TPU v7x, 32 devices: a whole 2x2x4 slice. The times are simulated.
32 devices in a mesh: seq: 8 (over z, x), tier: 4 (over y, core).
Axes of the slice: x: 2, y: 2, z: 4, core: 2. Of those that a mesh axis runs over, the one named last changes fastest.
Arguments:
- layer_input: bfloat16 [8, 512, 1024], P('seq', 'tier'), may hold values from -6 to 6
- memory: bfloat16 [8, 512, 1024], P('seq', 'tier'), may hold values from -6 to 6
- compressed: bfloat16 [8, 512, 1024], P('seq', 'tier'), may hold values from -6 to 6
- seg_len: int32 [8], P('seq'), may hold values from 1 to 512, as said below
- hist_len: int32 [8], P('seq'), may hold values from 0 to 1024, as said below
- query_weight: bfloat16 [1024, 1024], replicated, may hold values from -0.1875 to 0.1875
- key_weight: bfloat16 [1024, 1024], replicated, may hold values from -0.1875 to 0.1875
- value_weight: bfloat16 [1024, 1024], replicated, may hold values from -0.1875 to 0.1875
- attn_out_weight: bfloat16 [1024, 1024], replicated, may hold values from -1 to 1
- ffn_in_weight: bfloat16 [1024, 4096], replicated, may hold values from -0.1875 to 0.1875
- ffn_out_weight: bfloat16 [4096, 1024], replicated, may hold values from -0.09375 to 0.09375
- norm_gain: float32 [1024], replicated, may hold values from 0.1 to 1.9
- head_slope: float32 [8], replicated, may hold values from 0.0005 to 0.05
- comp_weight: bfloat16 [3072, 1024], replicated, may hold values from -0.109375 to 0.109375
- cotangent: bfloat16 [8, 512, 1024], P('seq', 'tier'), may hold values from -6 to 6
Outputs:
- output: bfloat16 [8, 512, 1024], P('seq', 'tier')
- grad_input: float32 [8, 512, 1024], P('seq', 'tier')
- new_memory: bfloat16 [8, 512, 1024], P('seq', 'tier')
- new_compressed: bfloat16 [8, 512, 1024], P('seq', 'tier')
- grad_query_weight: float32 [1024, 1024], P('seq', 'tier')
- grad_key_weight: float32 [1024, 1024], P('seq', 'tier')
- grad_value_weight: float32 [1024, 1024], P('seq', 'tier')
- grad_attn_out_weight: float32 [1024, 1024], P('seq', 'tier')
- grad_ffn_in_weight: float32 [1024, 4096], P('seq', 'tier')
- grad_ffn_out_weight: float32 [4096, 1024], P('seq', 'tier')
- grad_comp_weight: float32 [3072, 1024], P('seq', 'tier')
- grad_norm_gain: float32 [1024], replicated
- grad_head_slope: float32 [8], replicated
Inputs may be any that keep to these rules, and one draw needn't show every extreme that they name: `seg_len`: the first sequence's segment is full; others may end early, as the last segment of a book does. `hist_len`: the first sequence has a full history; a book's early segments have a short one.
All inputs are finite; a program needn't handle non-finite values.
Results may differ from a plain program's by a relative error of at most 0.014.
Values may be sent and summed in bfloat16 or wider, within the bound.
A program may use at most 256 MiB of HBM per device.

v0:
```python
import math

import jax
import jax.numpy as jnp
from jax import lax
from jax.sharding import PartitionSpec as P

norm_eps = 1e-05
neg_large = -1e30


def gelu_tanh(values_in):
    return jax.nn.gelu(values_in, approximate=True)


def layer_norm(residual, norm_gain):
    centre = jnp.mean(residual, axis=-1, keepdims=True)
    deviation = residual - centre
    variance = jnp.mean(deviation * deviation, axis=-1, keepdims=True)
    return deviation * lax.rsqrt(variance + norm_eps) * norm_gain


def softmax_stats(scores, key_valid):
    masked = jnp.where(key_valid, scores, neg_large)
    log_total = jax.nn.logsumexp(masked, axis=-1, keepdims=True)
    return jnp.exp(masked - log_total)


def softmax_grad(weights, grad_weights):
    inner_sum = jnp.sum(weights * grad_weights, axis=-1, keepdims=True)
    return (weights * (grad_weights - inner_sum)).astype(jnp.bfloat16)


def per_device(
    layer_input,
    memory,
    compressed,
    seg_len,
    hist_len,
    query_weight,
    key_weight,
    value_weight,
    attn_out_weight,
    ffn_in_weight,
    ffn_out_weight,
    norm_gain,
    head_slope,
    comp_weight,
    cotangent,
):
    seq_count, row_count, model_width = layer_input.shape
    tier_count = lax.axis_size("tier")
    tier_pos = lax.axis_index("tier")
    head_count = head_slope.shape[0]
    head_dim = model_width // head_count
    seg_rows = row_count * tier_count
    key_count = 3 * seg_rows
    comp_count = (seg_rows + 2) // 3
    per_tier = -(-comp_count // tier_count)
    win_total = per_tier * tier_count
    inv_root = 1.0 / math.sqrt(head_dim)
    row_ids = tier_pos * row_count + jnp.arange(row_count, dtype=jnp.int32)
    row_mask = (row_ids[None, :] < seg_len[:, None]).astype(jnp.float32)
    hidden_in = (layer_input.astype(jnp.float32) * row_mask[:, :, None]).astype(jnp.bfloat16)
    kv_weight = jnp.concatenate([key_weight, value_weight], axis=1)
    queries = jnp.einsum(
        "srd,de->sre", hidden_in, query_weight, preferred_element_type=jnp.float32
    ).astype(jnp.bfloat16)
    query_heads = queries.reshape(seq_count, row_count, head_count, head_dim)
    local_rows = jnp.stack([compressed, memory, hidden_in], axis=1)
    state_local = jnp.stack([compressed, memory], axis=1)
    kv_local = jnp.einsum(
        "strd,de->stre", local_rows, kv_weight, preferred_element_type=jnp.float32
    ).astype(jnp.bfloat16)
    kv_all, state_all = (
        lax.all_gather(kv_local, "tier", axis=2, tiled=True),
        lax.all_gather(state_local, "tier", axis=2, tiled=True),
    )
    kv_flat = kv_all.reshape(seq_count, key_count, 2 * model_width)
    mem_kv = kv_all[:, 1]
    key_heads = kv_flat[:, :, :model_width].reshape(seq_count, key_count, head_count, head_dim)
    value_heads = kv_flat[:, :, model_width:].reshape(seq_count, key_count, head_count, head_dim)
    key_ids = jnp.arange(key_count, dtype=jnp.int32)
    offsets = (2 * seg_rows + row_ids)[:, None] - key_ids[None, :]
    distance = offsets.astype(jnp.float32)
    in_history = (key_ids[None, :] < 2 * seg_rows) & (
        key_ids[None, :] >= 2 * seg_rows - hist_len[:, None]
    )
    in_segment = (key_ids[None, :] >= 2 * seg_rows) & (offsets >= 0)
    key_valid = in_history[:, None, None, :] | in_segment[None, None]
    scores = (
        jnp.einsum("srhd,skhd->shrk", query_heads, key_heads, preferred_element_type=jnp.float32)
        * inv_root
    )
    scores = scores - head_slope[None, :, None, None] * distance[None, None]
    weights_main = softmax_stats(scores, key_valid)
    weights_low = weights_main.astype(jnp.bfloat16)
    attended = jnp.einsum(
        "shrk,skhd->srhd", weights_low, value_heads, preferred_element_type=jnp.float32
    )
    attended = attended.reshape(seq_count, row_count, model_width).astype(jnp.bfloat16)
    attn_out = jnp.einsum(
        "srd,de->sre", attended, attn_out_weight, preferred_element_type=jnp.float32
    )
    residual = hidden_in.astype(jnp.float32) + attn_out
    normed, norm_pull = jax.vjp(layer_norm, residual, norm_gain)
    normed_low = normed.astype(jnp.bfloat16)
    pre_act = jnp.einsum(
        "srd,df->srf", normed_low, ffn_in_weight, preferred_element_type=jnp.float32
    )
    act_value, gelu_pull = jax.vjp(gelu_tanh, pre_act)
    activation = act_value.astype(jnp.bfloat16)
    ffn_result = jnp.einsum(
        "srf,fd->srd", activation, ffn_out_weight, preferred_element_type=jnp.float32
    )
    output = ((residual + ffn_result) * row_mask[:, :, None]).astype(jnp.bfloat16)
    memory_all = state_all[:, 1]
    padded = jnp.pad(memory_all, ((0, 0), (0, 3 * win_total - seg_rows), (0, 0)))
    windows_own = lax.dynamic_slice_in_dim(padded, tier_pos * 3 * per_tier, 3 * per_tier, axis=1)
    windows_own = windows_own.reshape(seq_count, per_tier, 3 * model_width)
    comp_own = jnp.einsum(
        "swc,cd->swd", windows_own, comp_weight, preferred_element_type=jnp.float32
    ).astype(jnp.bfloat16)
    kvc_own = jnp.einsum(
        "swd,de->swe", comp_own, kv_weight, preferred_element_type=jnp.float32
    ).astype(jnp.bfloat16)
    kvc_all, comp_all = (
        lax.all_gather(kvc_own, "tier", axis=1, tiled=True),
        lax.all_gather(comp_own, "tier", axis=1, tiled=True),
    )
    merged_state = jnp.concatenate([state_all[:, 0, comp_count:], comp_all[:, :comp_count]], axis=1)
    new_compressed = lax.dynamic_slice_in_dim(merged_state, tier_pos * row_count, row_count, axis=1)
    mem_keys = mem_kv[:, :, :model_width].reshape(seq_count, seg_rows, head_count, head_dim)
    mem_values = mem_kv[:, :, model_width:].reshape(seq_count, seg_rows, head_count, head_dim)
    mem_scores = (
        jnp.einsum("srhd,skhd->shrk", query_heads, mem_keys, preferred_element_type=jnp.float32)
        * inv_root
    )
    mem_weights = jax.nn.softmax(mem_scores, axis=-1).astype(jnp.bfloat16)
    from_memory = jnp.einsum(
        "shrk,skhd->srhd", mem_weights, mem_values, preferred_element_type=jnp.float32
    )
    comp_keys = kvc_all[:, :, :model_width].reshape(seq_count, win_total, head_count, head_dim)
    comp_values = kvc_all[:, :, model_width:].reshape(seq_count, win_total, head_count, head_dim)
    comp_valid = (jnp.arange(win_total, dtype=jnp.int32) < comp_count)[None, None, None, :]
    comp_scores = (
        jnp.einsum("srhd,skhd->shrk", query_heads, comp_keys, preferred_element_type=jnp.float32)
        * inv_root
    )
    comp_weights = softmax_stats(comp_scores, comp_valid)
    comp_low = comp_weights.astype(jnp.bfloat16)
    from_comp = jnp.einsum(
        "shrk,skhd->srhd", comp_low, comp_values, preferred_element_type=jnp.float32
    )
    grad_comp_out = ((from_comp - from_memory) * row_mask[:, :, None, None]).astype(jnp.bfloat16)
    grad_comp_weights = jnp.einsum(
        "srhd,skhd->shrk", grad_comp_out, comp_values, preferred_element_type=jnp.float32
    )
    grad_comp_scores = softmax_grad(comp_weights, grad_comp_weights)
    grad_comp_keys = (
        jnp.einsum(
            "shrk,srhd->skhd", grad_comp_scores, query_heads, preferred_element_type=jnp.float32
        )
        * inv_root
    )
    grad_comp_values = jnp.einsum(
        "shrk,srhd->skhd", comp_low, grad_comp_out, preferred_element_type=jnp.float32
    )
    grad_kvc = jnp.concatenate(
        [
            grad_comp_keys.reshape(seq_count, win_total, model_width),
            grad_comp_values.reshape(seq_count, win_total, model_width),
        ],
        axis=-1,
    )
    grad_rows = cotangent.astype(jnp.float32) * row_mask[:, :, None]
    grad_low = grad_rows.astype(jnp.bfloat16)
    part_ffn_out = jnp.einsum(
        "srf,srd->fd", activation, grad_low, preferred_element_type=jnp.float32
    )
    grad_act = jnp.einsum(
        "srd,fd->srf", grad_low, ffn_out_weight, preferred_element_type=jnp.float32
    )
    grad_pre = gelu_pull(grad_act)[0].astype(jnp.bfloat16)
    part_ffn_in = jnp.einsum(
        "srd,srf->df", normed_low, grad_pre, preferred_element_type=jnp.float32
    )
    grad_normed = jnp.einsum(
        "srf,df->srd", grad_pre, ffn_in_weight, preferred_element_type=jnp.float32
    )
    grad_resid_norm, part_gain = norm_pull(grad_normed)
    grad_resid = grad_rows + grad_resid_norm
    grad_attn_low = grad_resid.astype(jnp.bfloat16)
    part_attn_out = jnp.einsum(
        "srd,sre->de", attended, grad_attn_low, preferred_element_type=jnp.float32
    )
    grad_attended = jnp.einsum(
        "sre,de->srd", grad_attn_low, attn_out_weight, preferred_element_type=jnp.float32
    ).astype(jnp.bfloat16)
    grad_att_heads = grad_attended.reshape(seq_count, row_count, head_count, head_dim)
    grad_weights = jnp.einsum(
        "srhd,skhd->shrk", grad_att_heads, value_heads, preferred_element_type=jnp.float32
    )
    grad_scores = softmax_grad(weights_main, grad_weights)
    part_slope = -jnp.einsum("shrk,rk->h", grad_scores.astype(jnp.float32), distance)
    grad_queries = (
        jnp.einsum("shrk,skhd->srhd", grad_scores, key_heads, preferred_element_type=jnp.float32)
        * inv_root
    )
    grad_queries = grad_queries.reshape(seq_count, row_count, model_width).astype(jnp.bfloat16)
    grad_keys = (
        jnp.einsum("shrk,srhd->skhd", grad_scores, query_heads, preferred_element_type=jnp.float32)
        * inv_root
    )
    grad_values = jnp.einsum(
        "shrk,srhd->skhd", weights_low, grad_att_heads, preferred_element_type=jnp.float32
    )
    grad_kv = jnp.concatenate(
        [
            grad_keys.reshape(seq_count, 3, seg_rows, model_width),
            grad_values.reshape(seq_count, 3, seg_rows, model_width),
        ],
        axis=-1,
    )
    kv_grad_own, kvc_grad_own = (
        lax.psum_scatter(grad_kv, "tier", scatter_dimension=2, tiled=True),
        lax.psum_scatter(grad_kvc, "tier", scatter_dimension=1, tiled=True),
    )
    kv_grad_low = kv_grad_own.astype(jnp.bfloat16)
    kvc_grad_low = kvc_grad_own.astype(jnp.bfloat16)
    part_kv = jnp.einsum(
        "strd,stre->de", local_rows, kv_grad_low, preferred_element_type=jnp.float32
    )
    part_query = jnp.einsum(
        "srd,sre->de", hidden_in, grad_queries, preferred_element_type=jnp.float32
    )
    grad_hidden = grad_resid + jnp.einsum(
        "sre,de->srd", grad_queries, query_weight, preferred_element_type=jnp.float32
    )
    grad_hidden = grad_hidden + jnp.einsum(
        "sre,de->srd", kv_grad_low[:, 2], kv_weight, preferred_element_type=jnp.float32
    )
    grad_input = grad_hidden * row_mask[:, :, None]
    grad_comp = jnp.einsum(
        "swe,de->swd", kvc_grad_low, kv_weight, preferred_element_type=jnp.float32
    ).astype(jnp.bfloat16)
    part_comp = jnp.einsum(
        "swc,swd->cd", windows_own, grad_comp, preferred_element_type=jnp.float32
    )
    part_key = part_kv[:, :model_width]
    part_value = part_kv[:, model_width:]
    section_one = (
        lax.psum_scatter(part_query, "tier", scatter_dimension=1, tiled=True),
        lax.psum_scatter(part_key, "tier", scatter_dimension=1, tiled=True),
        lax.psum_scatter(part_value, "tier", scatter_dimension=1, tiled=True),
        lax.psum_scatter(part_attn_out, "tier", scatter_dimension=1, tiled=True),
        lax.psum_scatter(part_ffn_in, "tier", scatter_dimension=1, tiled=True),
        lax.psum_scatter(part_ffn_out, "tier", scatter_dimension=1, tiled=True),
        lax.psum_scatter(part_comp, "tier", scatter_dimension=1, tiled=True),
    )
    reduced = (
        lax.psum_scatter(section_one[0], "seq", scatter_dimension=0, tiled=True),
        lax.psum_scatter(section_one[1], "seq", scatter_dimension=0, tiled=True),
        lax.psum_scatter(section_one[2], "seq", scatter_dimension=0, tiled=True),
        lax.psum_scatter(section_one[3], "seq", scatter_dimension=0, tiled=True),
        lax.psum_scatter(section_one[4], "seq", scatter_dimension=0, tiled=True),
        lax.psum_scatter(section_one[5], "seq", scatter_dimension=0, tiled=True),
        lax.psum_scatter(section_one[6], "seq", scatter_dimension=0, tiled=True),
    )
    gain_total, slope_total = lax.psum((part_gain, part_slope), ("seq", "tier"))
    return (
        output,
        grad_input,
        hidden_in,
        new_compressed,
        reduced[0],
        reduced[1],
        reduced[2],
        reduced[3],
        reduced[4],
        reduced[5],
        reduced[6],
        gain_total,
        slope_total,
    )


def solution(mesh):
    placed = (
        P("seq", "tier", None),
        P("seq", "tier", None),
        P("seq", "tier", None),
        P("seq"),
        P("seq"),
        P(),
        P(),
        P(),
        P(),
        P(),
        P(),
        P(),
        P(),
        P(),
        P("seq", "tier", None),
    )
    return jax.shard_map(
        per_device,
        mesh=mesh,
        in_specs=placed,
        out_specs=(
            P("seq", "tier", None),
            P("seq", "tier", None),
            P("seq", "tier", None),
            P("seq", "tier", None),
            P("seq", "tier"),
            P("seq", "tier"),
            P("seq", "tier"),
            P("seq", "tier"),
            P("seq", "tier"),
            P("seq", "tier"),
            P("seq", "tier"),
            P(),
            P(),
        ),
        check_vma=False,
    )
```

profile of v0, /device:TPU:0, one launch (start us, length us, event | category | flops | bytes accessed | tf_op | source)
XLA Modules:
  0.0 1536.5 jit_solution(75846250421366016)
XLA Ops:
  14.6 5.2 fusion.4
  25.6 43.4 %all-gather.10.cloned.1.call-done = bf16[3,512,2048]{2,1,0:T(8,128)(2,1)} async-done(((bf16[3,128,2048]{2,1,0:T(8,128)(2,1)}), bf16[3,512,2048]{2,1,0:T(8,128)(2,1)}) %all-gather.10.cloned.1.call-update) | async-done | bytes 6291472 | tf_op jit(solution)/shard_map/all_gather | solution.py:76
  69.0 6.2 fusion.107
  79.9 4.8 copy.91
  107.7 5.7 multiply_reduce_fusion.1
  113.4 6.6 convolution_bitcast_fusion.1
  127.9 6.6 copy.100
  134.5 6.6 copy.98
  141.1 46.0 %bitcast_reduce_fusion = f32[512,3,2048]{2,1,0:T(4,128)} fusion(f32[1,3,512,1024]{3,0,2,1:T(1,128)} %bitcast.228, f32[1,3,512,1024]{3,0,2,1:T(1,128)} %bitcast.229), kind=kLoop, calls=%fused_computation.2 | loop fusion | flops 3145728 | bytes 25165824
  187.1 22.8 %copy.134 = f32[64,8,3,2048]{3,1,2,0:T(8,128)} copy(f32[64,8,3,2048]{3,2,1,0:T(4,128)} %bitcast.222) | data formatting | bytes 25165824
  225.5 5.2 convolution_convert_fusion.5
  232.2 8.6 all-gather.4
  256.2 282.3 %all-reduce.4 = bf16[1,172,2048]{2,0,1:T(2,128)(2,1)} all-reduce(f32[1,172,2048]{2,0,1:T(1,128)S(1)} %pad_maximum_fusion.1), channel_id=18, replica_groups=mesh['seq'=8,'tier'=4] {'tier'}, use_global_device_ids=true, to_apply=%region_25.26.clone | all-reduce | flops 352256 | bytes 2113536
  539.9 9.7 fusion.32
  549.6 7.1 reshape.602
  562.1 5.6 fusion.106
  569.7 8.2 fusion.75
  579.4 8.2 fusion.101
  589.0 60.9 %reduce-scatter.43.cloned.1.call-done = f32[3072,256]{1,0:T(8,128)} async-done(((f32[3072,1024]{1,0:T(8,128)}), f32[3072,256]{1,0:T(8,128)}) %reduce-scatter.43.cloned.1.call-update) | async-done | bytes 3145744 | tf_op jit(solution)/shard_map/reduce_scatter | solution.py:259
  649.9 47.0 %reduce-scatter.27.cloned.1.call-done = f32[1024,256]{1,0:T(8,128)} async-done(((f32[1024,1024]{1,0:T(8,128)}), f32[1024,256]{1,0:T(8,128)}) %reduce-scatter.27.cloned.1.call-update) | async-done | bytes 1048592 | tf_op jit(solution)/shard_map/reduce_scatter | solution.py:255
  697.0 47.1 %reduce-scatter.23.cloned.1.call-done = f32[1024,256]{1,0:T(8,128)} async-done(((f32[1024,1024]{1,0:T(8,128)}), f32[1024,256]{1,0:T(8,128)}) %reduce-scatter.23.cloned.1.call-update) | async-done | bytes 1048592 | tf_op jit(solution)/shard_map/reduce_scatter | solution.py:254
  744.2 128.7 %reduce-scatter.39.cloned.1.call-done = f32[4096,256]{1,0:T(8,128)} async-done(((f32[4096,1024]{1,0:T(8,128)}), f32[4096,256]{1,0:T(8,128)}) %reduce-scatter.39.cloned.1.call-update) | async-done | bytes 4194320 | tf_op jit(solution)/shard_map/reduce_scatter | solution.py:258
  873.0 128.7 %reduce-scatter.35.cloned.1.call-done = f32[1024,1024]{1,0:T(8,128)} async-done(((f32[1024,4096]{1,0:T(8,128)}), f32[1024,1024]{1,0:T(8,128)}) %reduce-scatter.35.cloned.1.call-update) | async-done | bytes 4194320 | tf_op jit(solution)/shard_map/reduce_scatter | solution.py:257
  1001.7 6.7 all-gather.3
  1012.6 41.0 %all-reduce.2 = (f32[1024]{0:T(1024)}, f32[8]{0:T(128)}) all-reduce(f32[1024]{0:T(1024)S(1)} %get-tuple-element.13, f32[8]{0:T(128)S(1)} %neg.7), channel_id=1, replica_groups=mesh['seq'=8,'tier'=4] {'seq','tier'}, use_global_device_ids=true, to_apply=%region_29.30 | all-reduce | flops 1032 | bytes 8256 | tf_op jit(solution)/shard_map/psum | solution.py:270
  1055.4 6.5 fusion.27
  1069.2 66.6 %reduce-scatter.21.cloned.1.call-done = f32[128,256]{1,0:T(8,128)} async-done(((f32[1024,256]{1,0:T(8,128)}), f32[128,256]{1,0:T(8,128)}) %reduce-scatter.21.cloned.1.call-update) | async-done | bytes 131088 | tf_op jit(solution)/shard_map/reduce_scatter | solution.py:262
  1135.8 77.5 %reduce-scatter.45.cloned.1.call-done = f32[384,256]{1,0:T(8,128)} async-done(((f32[3072,256]{1,0:T(8,128)}), f32[384,256]{1,0:T(8,128)}) %reduce-scatter.45.cloned.1.call-update) | async-done | bytes 393232 | tf_op jit(solution)/shard_map/reduce_scatter | solution.py:268
  1213.3 66.3 %reduce-scatter.29.cloned.1.call-done = f32[128,256]{1,0:T(8,128)} async-done(((f32[1024,256]{1,0:T(8,128)}), f32[128,256]{1,0:T(8,128)}) %reduce-scatter.29.cloned.1.call-update) | async-done | bytes 131088 | tf_op jit(solution)/shard_map/reduce_scatter | solution.py:264
  1279.6 66.6 %reduce-scatter.25.cloned.1.call-done = f32[128,256]{1,0:T(8,128)} async-done(((f32[1024,256]{1,0:T(8,128)}), f32[128,256]{1,0:T(8,128)}) %reduce-scatter.25.cloned.1.call-update) | async-done | bytes 131088 | tf_op jit(solution)/shard_map/reduce_scatter | solution.py:263
  1346.3 91.0 %reduce-scatter.41.cloned.1.call-done = f32[512,256]{1,0:T(8,128)} async-done(((f32[4096,256]{1,0:T(8,128)}), f32[512,256]{1,0:T(8,128)}) %reduce-scatter.41.cloned.1.call-update) | async-done | bytes 524304 | tf_op jit(solution)/shard_map/reduce_scatter | solution.py:267
  1437.2 92.2 %reduce-scatter.37.cloned.1.call-done = f32[128,1024]{1,0:T(8,128)} async-done(((f32[1024,1024]{1,0:T(8,128)}), f32[128,1024]{1,0:T(8,128)}) %reduce-scatter.37.cloned.1.call-update) | async-done | bytes 524304 | tf_op jit(solution)/shard_map/reduce_scatter | solution.py:266
  (203 shorter events, 103.6 us)
Async XLA Ops:
  7.2 85.8 %copy-start = (bf16[1024,1024]{1,0:T(8,128)(2,1)S(1)}, bf16[1024,1024]{1,0:T(8,128)(2,1)}, u32[]{:S(2)}) copy-start(bf16[1024,1024]{1,0:T(8,128)(2,1)} %param.23) | copy-start | bytes 6291460
  7.2 61.8 %all-gather.10.cloned.1.call-start = ((), (), s32[]{:S(2)}) async-start(), calls=%async_computation.30 | async-start | bytes 7864320 | tf_op jit(solution)/shard_map/all_gather | solution.py:76
  19.8 203.9 %all-gather.8.cloned.1.call-start = ((), (), s32[]{:S(2)}) async-start(), calls=%async_computation.15 | async-start | bytes 2621440 | tf_op jit(solution)/shard_map/all_gather | solution.py:77
  20.7 529.0 %reduce-scatter.47.cloned.1.call-start = ((), (), s32[]{:S(2)}) async-start(), calls=%async_computation.31 | async-start | bytes 15728640
  20.8 197.5 %copy-start.13 = (bf16[1,128,1024]{2,1,0:T(8,128)(2,1)}, bf16[1,128,1024]{2,1,0:T(8,128)(2,1)S(1)}, u32[]{:S(2)}) copy-start(bf16[1,128,1024]{2,1,0:T(8,128)(2,1)S(1)} %multiply_convert_fusion.4) | copy-start | bytes 786436
  25.6 59.1 %copy-start.17 = (bf16[16,8,8,128]{3,2,1,0:T(8,128)(2,1)}, bf16[16,8,8,128]{3,2,1,0:T(8,128)(2,1)S(1)}, u32[]{:S(2)}) copy-start(bf16[16,8,8,128]{3,2,1,0:T(8,128)(2,1)S(1)} %fusion.30) | copy-start | bytes 786436
  79.9 4.8 copy-start.36
  84.7 7.1 copy-start.5
  88.6 5.1 slice-start.2
  107.6 12.4 slice-start
  107.6 12.4 slice-start.1
  113.4 6.6 copy-start.14
  120.0 4.3 copy-start.18
  209.9 377.8 %reduce-scatter.31.cloned.1.call-start = ((), (), s32[]{:S(2)}) async-start(), calls=%async_computation.22 | async-start | bytes 5242880 | tf_op jit(solution)/shard_map/reduce_scatter | solution.py:256
  213.6 374.9 %reduce-scatter.19.cloned.1.call-start = ((), (), s32[]{:S(2)}) async-start(), calls=%async_computation.16 | async-start | bytes 5242880 | tf_op jit(solution)/shard_map/reduce_scatter | solution.py:253
  221.7 428.1 %reduce-scatter.43.cloned.1.call-start = ((), (), s32[]{:S(2)}) async-start(), calls=%async_computation.28 | async-start | bytes 15728640 | tf_op jit(solution)/shard_map/reduce_scatter | solution.py:259
  225.5 5.9 copy-start.3
  549.6 147.4 %reduce-scatter.27.cloned.1.call-start = ((), (), s32[]{:S(2)}) async-start(), calls=%async_computation.20 | async-start | bytes 5242880 | tf_op jit(solution)/shard_map/reduce_scatter | solution.py:255
  567.8 176.3 %reduce-scatter.23.cloned.1.call-start = ((), (), s32[]{:S(2)}) async-start(), calls=%async_computation.18 | async-start | bytes 5242880 | tf_op jit(solution)/shard_map/reduce_scatter | solution.py:254
  568.5 304.4 %reduce-scatter.39.cloned.1.call-start = ((), (), s32[]{:S(2)}) async-start(), calls=%async_computation.26 | async-start | bytes 20971520 | tf_op jit(solution)/shard_map/reduce_scatter | solution.py:258
  577.9 423.8 %reduce-scatter.35.cloned.1.call-start = ((), (), s32[]{:S(2)}) async-start(), calls=%async_computation.24 | async-start | bytes 20971520 | tf_op jit(solution)/shard_map/reduce_scatter | solution.py:257
  587.6 481.6 %reduce-scatter.33.cloned.1.call-start = ((), (), s32[]{:S(2)}) async-start(), calls=%async_computation.23 | async-start | bytes 1179648 | tf_op jit(solution)/shard_map/reduce_scatter | solution.py:265
  588.4 547.5 %reduce-scatter.21.cloned.1.call-start = ((), (), s32[]{:S(2)}) async-start(), calls=%async_computation.17 | async-start | bytes 1179648 | tf_op jit(solution)/shard_map/reduce_scatter | solution.py:262
  588.9 624.4 %reduce-scatter.45.cloned.1.call-start = ((), (), s32[]{:S(2)}) async-start(), calls=%async_computation.29 | async-start | bytes 3538944 | tf_op jit(solution)/shard_map/reduce_scatter | solution.py:268
  649.9 629.8 %reduce-scatter.29.cloned.1.call-start = ((), (), s32[]{:S(2)}) async-start(), calls=%async_computation.21 | async-start | bytes 1179648 | tf_op jit(solution)/shard_map/reduce_scatter | solution.py:264
  696.9 649.3 %reduce-scatter.25.cloned.1.call-start = ((), (), s32[]{:S(2)}) async-start(), calls=%async_computation.19 | async-start | bytes 1179648 | tf_op jit(solution)/shard_map/reduce_scatter | solution.py:263
  744.2 693.1 %reduce-scatter.41.cloned.1.call-start = ((), (), s32[]{:S(2)}) async-start(), calls=%async_computation.27 | async-start | bytes 4718592 | tf_op jit(solution)/shard_map/reduce_scatter | solution.py:267
  873.0 128.8 %copy-start.34 = (bf16[43,1024]{1,0:T(8,128)(2,1)S(1)}, bf16[43,1024]{1,0:T(8,128)(2,1)}, u32[]{:S(2)}) copy-start(bf16[43,1024]{1,0:T(8,128)(2,1)} %copy-done.33) | copy-start | bytes 264196
  873.0 656.5 %reduce-scatter.37.cloned.1.call-start = ((), (), s32[]{:S(2)}) async-start(), calls=%async_computation.25 | async-start | bytes 4718592 | tf_op jit(solution)/shard_map/reduce_scatter | solution.py:266
  1001.7 51.9 %copy-start.10 = (bf16[1024,1024]{1,0:T(8,128)(2,1)S(1)}, bf16[1024,1024]{1,0:T(8,128)(2,1)}, u32[]{:S(2)}) copy-start(bf16[1024,1024]{1,0:T(8,128)(2,1)} %param.20) | copy-start | bytes 6291460
  1055.4 6.5 copy-start.4
  1055.4 474.1 %copy-start.1 = (bf16[1024,1024]{1,0:T(8,128)(2,1)S(1)}, bf16[1024,1024]{1,0:T(8,128)(2,1)}, u32[]{:S(2)}) copy-start(bf16[1024,1024]{1,0:T(8,128)(2,1)} %param.23) | copy-start | bytes 6291460
  (29 other events, 68.9 us)
Sparse Core Ops, SparseCore 0:
  19.9 49.0 all-gather.9
  71.1 22.5 all-gather.7
  210.0 143.8 reduce-scatter.46
  356.3 65.6 reduce-scatter.30
  424.6 67.2 reduce-scatter.18
  549.7 100.1 reduce-scatter.42
  652.4 44.4 reduce-scatter.26
  699.6 44.4 reduce-scatter.22
  746.7 126.1 reduce-scatter.38
  875.5 126.1 reduce-scatter.34
  1005.7 63.4 reduce-scatter.32
  1073.4 62.3 reduce-scatter.20
  1140.0 73.2 reduce-scatter.44
  1217.2 62.4 reduce-scatter.28
  1283.8 62.3 reduce-scatter.24
  1350.3 86.8 reduce-scatter.40
  1441.7 87.6 reduce-scatter.36
where the time goes:
time: 1540 us
  waiting for transfers between devices  922 us (60%)
  blocking collectives  339 us (22%)
  matrix products  103 us (7%)
  local copies, waits for them, and re-layouts  98.8 us (6%)
  other arithmetic  55.7 us (4%)
  between operations  17.4 us (1%)
    unnamed x1, blocking collectives  282 us
    reduce_scatter x1, waiting for transfers between devices, per_device(): lax.psum_scatter(part_ffn_out, 'tier', scatter_dimension=1, tiled=True)  129 us
    reduce_scatter x1, waiting for transfers between devices, per_device(): lax.psum_scatter(part_ffn_in, 'tier', scatter_dimension=1, tiled=True)  129 us
    reduce_scatter x1, waiting for transfers between devices, per_device(): lax.psum_scatter(section_one[4], 'seq', scatter_dimension=0, tiled=True)  92.2 us
    reduce_scatter x1, waiting for transfers between devices, per_device(): lax.psum_scatter(section_one[5], 'seq', scatter_dimension=0, tiled=True)  91 us
    reduce_scatter x1, waiting for transfers between devices, per_device(): lax.psum_scatter(section_one[6], 'seq', scatter_dimension=0, tiled=True)  77.5 us
    reduce_scatter x1, waiting for transfers between devices, per_device(): lax.psum_scatter(section_one[0], 'seq', scatter_dimension=0, tiled=True)  66.6 us
    reduce_scatter x1, waiting for transfers between devices, per_device(): lax.psum_scatter(section_one[1], 'seq', scatter_dimension=0, tiled=True)  66.6 us
  transfers between devices with their start and end apart: 17, of which 13 were waited for; matrix products, arithmetic and copies ran while one was open for 15% of the time, Pallas kernels for 0%

commit v1 on v0

v1 whole, which is shorter than its diff:
```python
import math

import jax
import jax.numpy as jnp
from jax import lax
from jax.sharding import PartitionSpec as P

norm_eps = 1e-05
neg_large = -1e30
f32 = jnp.float32
bf16 = jnp.bfloat16


def gelu_tanh(values_in):
    return jax.nn.gelu(values_in, approximate=True)


def layer_norm(residual, norm_gain):
    centre = jnp.mean(residual, axis=-1, keepdims=True)
    deviation = residual - centre
    variance = jnp.mean(deviation * deviation, axis=-1, keepdims=True)
    return deviation * lax.rsqrt(variance + norm_eps) * norm_gain


def softmax_grad(weights, grad_weights):
    inner_sum = jnp.sum(weights * grad_weights, axis=-1, keepdims=True)
    return (weights * (grad_weights - inner_sum)).astype(bf16)


def mm(left, right):
    return jnp.dot(left, right, preferred_element_type=f32)


def mm_tn(left, right):
    return lax.dot_general(left, right, (((0,), (0,)), ((), ())), preferred_element_type=f32)


def mm_nt(left, right):
    return lax.dot_general(left, right, (((1,), (1,)), ((), ())), preferred_element_type=f32)


def per_device(
    layer_input,
    memory,
    compressed,
    seg_len,
    hist_len,
    query_weight,
    key_weight,
    value_weight,
    attn_out_weight,
    ffn_in_weight,
    ffn_out_weight,
    norm_gain,
    head_slope,
    comp_weight,
    cotangent,
):
    _, row_count, width = layer_input.shape
    tiers = lax.axis_size("tier")
    seqs = lax.axis_size("seq")
    tier_pos = lax.axis_index("tier")
    heads = head_slope.shape[0]
    head_dim = width // heads
    hpt = heads // tiers
    cb = hpt * head_dim
    ff = ffn_in_weight.shape[1]
    ffb = ff // tiers
    seg = row_count * tiers
    keys_n = 3 * seg
    ncomp = (seg + 2) // 3
    inv_root = 1.0 / math.sqrt(head_dim)
    length = seg_len[0]
    history = hist_len[0]

    own_ids = tier_pos * row_count + jnp.arange(row_count, dtype=jnp.int32)
    mask_own = (own_ids < length).astype(f32)[:, None]
    all_ids = jnp.arange(seg, dtype=jnp.int32)
    mask_all = (all_ids < length).astype(f32)[:, None]

    hidden_own = (layer_input[0].astype(f32) * mask_own).astype(bf16)
    raw_local = jnp.stack([compressed[0], memory[0], hidden_own], axis=0)
    raw_seq = lax.all_gather(raw_local, "tier", axis=1, tiled=True)
    cot_seq = lax.all_gather(cotangent[0], "tier", axis=0, tiled=True)
    context = raw_seq.reshape(keys_n, width)
    comp_rows = raw_seq[0]
    memory_rows = raw_seq[1]
    hidden_seq = raw_seq[2]

    col0 = tier_pos * cb
    wq_t = lax.dynamic_slice_in_dim(query_weight, col0, cb, axis=1)
    wk_t = lax.dynamic_slice_in_dim(key_weight, col0, cb, axis=1)
    wv_t = lax.dynamic_slice_in_dim(value_weight, col0, cb, axis=1)
    wkv_t = jnp.concatenate([wk_t, wv_t], axis=1)
    slope_t = lax.dynamic_slice_in_dim(head_slope, tier_pos * hpt, hpt)

    q_t = mm(hidden_seq, wq_t).astype(bf16)
    kv_t = mm(context, wkv_t).astype(bf16)
    q_h = q_t.reshape(seg, hpt, head_dim)
    k_h = kv_t[:, :cb].reshape(keys_n, hpt, head_dim)
    v_h = kv_t[:, cb:].reshape(keys_n, hpt, head_dim)

    key_ids = jnp.arange(keys_n, dtype=jnp.int32)
    offsets = (2 * seg + all_ids)[:, None] - key_ids[None, :]
    distance = offsets.astype(f32)
    in_history = (key_ids[None, :] < 2 * seg) & (key_ids[None, :] >= 2 * seg - history)
    in_segment = (key_ids[None, :] >= 2 * seg) & (offsets >= 0)
    key_valid = (in_history | in_segment)[None]
    scores = jnp.einsum("rhd,khd->hrk", q_h, k_h, preferred_element_type=f32) * inv_root
    scores = scores - slope_t[:, None, None] * distance[None]
    masked = jnp.where(key_valid, scores, neg_large)
    log_total = jax.nn.logsumexp(masked, axis=-1, keepdims=True)
    probs = jnp.exp(masked - log_total)
    probs_low = probs.astype(bf16)
    attended_t = jnp.einsum("hrk,khd->rhd", probs_low, v_h, preferred_element_type=f32)
    attended_t = attended_t.reshape(seg, cb).astype(bf16)
    attended = lax.all_to_all(attended_t, "tier", 0, 1, tiled=True)

    mem_k = k_h[seg : 2 * seg]
    mem_v = v_h[seg : 2 * seg]
    mem_scores = jnp.einsum("rhd,khd->hrk", q_h, mem_k, preferred_element_type=f32) * inv_root
    mem_probs = jax.nn.softmax(mem_scores, axis=-1).astype(bf16)
    from_memory = jnp.einsum("hrk,khd->rhd", mem_probs, mem_v, preferred_element_type=f32)
    padded = jnp.pad(memory_rows, ((0, 3 * ncomp - seg), (0, 0)))
    windows = padded.reshape(ncomp, 3 * width)
    comp_new = mm(windows, comp_weight).astype(bf16)
    ckv_t = mm(comp_new, wkv_t).astype(bf16)
    comp_k = ckv_t[:, :cb].reshape(ncomp, hpt, head_dim)
    comp_v = ckv_t[:, cb:].reshape(ncomp, hpt, head_dim)
    comp_scores = jnp.einsum("rhd,khd->hrk", q_h, comp_k, preferred_element_type=f32) * inv_root
    comp_probs = jax.nn.softmax(comp_scores, axis=-1)
    comp_low = comp_probs.astype(bf16)
    from_comp = jnp.einsum("hrk,khd->rhd", comp_low, comp_v, preferred_element_type=f32)
    grad_fc = ((from_comp - from_memory) * mask_all[:, :, None]).astype(bf16)
    grad_cw = jnp.einsum("rhd,khd->hrk", grad_fc, comp_v, preferred_element_type=f32)
    grad_cs = softmax_grad(comp_probs, grad_cw)
    grad_ck = (
        jnp.einsum("hrk,rhd->khd", grad_cs, q_h, preferred_element_type=f32) * inv_root
    ).astype(bf16)
    grad_cv = jnp.einsum("hrk,rhd->khd", comp_low, grad_fc, preferred_element_type=f32).astype(bf16)
    grad_ckv = jnp.concatenate(
        [grad_ck.reshape(ncomp, cb), grad_cv.reshape(ncomp, cb)], axis=1
    )
    grad_comp_part = mm_nt(grad_ckv, wkv_t)
    grad_comp_t = lax.psum_scatter(grad_comp_part, "tier", scatter_dimension=1, tiled=True)
    grad_comp_t = grad_comp_t.astype(bf16)
    part_comp = mm_tn(windows, grad_comp_t)

    full_comp = jnp.concatenate([comp_rows[ncomp:], comp_new[:ncomp]], axis=0)
    new_compressed = lax.dynamic_slice_in_dim(full_comp, tier_pos * row_count, row_count, axis=0)

    hidden_f = hidden_own.astype(f32)
    residual = hidden_f + mm(attended, attn_out_weight)
    normed, norm_pull = jax.vjp(layer_norm, residual, norm_gain)
    normed_low = normed.astype(bf16)
    pre_act = mm(normed_low, ffn_in_weight)
    act_value, gelu_pull = jax.vjp(gelu_tanh, pre_act)
    activation = act_value.astype(bf16)
    ffn_result = mm(activation, ffn_out_weight)
    output = ((residual + ffn_result) * mask_own).astype(bf16)

    grad_rows = cotangent[0].astype(f32) * mask_own
    grad_low = grad_rows.astype(bf16)
    grad_act = mm_nt(grad_low, ffn_out_weight)
    grad_pre = gelu_pull(grad_act)[0].astype(bf16)
    grad_normed = mm_nt(grad_pre, ffn_in_weight)
    grad_resid_norm, part_gain = norm_pull(grad_normed)
    grad_resid = grad_rows + grad_resid_norm
    grad_att = grad_resid.astype(bf16)
    grad_attended = mm_nt(grad_att, attn_out_weight).astype(bf16)
    back_t = lax.all_to_all(jnp.stack([grad_attended, grad_att], axis=0), "tier", 2, 1, tiled=True)
    grad_attended_t = back_t[0]
    grad_att_t = back_t[1]

    fwd_seq = lax.all_gather(jnp.stack([normed_low, attended], axis=0), "tier", axis=1, tiled=True)
    normed_seq = fwd_seq[0]
    attended_seq = fwd_seq[1]
    grad_seq = (cot_seq.astype(f32) * mask_all).astype(bf16)
    pre_seq = mm(normed_seq, ffn_in_weight)
    act_seq = gelu_tanh(pre_seq).astype(bf16)
    fcol0 = tier_pos * ffb
    pre_seq_t = lax.dynamic_slice_in_dim(pre_seq, fcol0, ffb, axis=1)
    wfo_t = lax.dynamic_slice_in_dim(ffn_out_weight, fcol0, ffb, axis=0)
    grad_act_seq_t = mm_nt(grad_seq, wfo_t)
    _, gelu_pull_seq = jax.vjp(gelu_tanh, pre_seq_t)
    grad_pre_seq_t = gelu_pull_seq(grad_act_seq_t)[0].astype(bf16)
    grad_seq_t = lax.dynamic_slice_in_dim(grad_seq, col0, cb, axis=1)
    part_ffn_in = mm_tn(normed_seq, grad_pre_seq_t)
    part_ffn_out = mm_tn(act_seq, grad_seq_t)
    part_attn_out = mm_tn(attended_seq, grad_att_t)

    grad_att_h = grad_attended_t.reshape(seg, hpt, head_dim)
    grad_probs = jnp.einsum("rhd,khd->hrk", grad_att_h, v_h, preferred_element_type=f32)
    grad_scores = softmax_grad(probs, grad_probs)
    part_slope = -jnp.einsum("hrk,rk->h", grad_scores.astype(f32), distance)
    grad_q = (
        jnp.einsum("hrk,khd->rhd", grad_scores, k_h, preferred_element_type=f32) * inv_root
    ).reshape(seg, cb).astype(bf16)
    grad_k = (
        jnp.einsum("hrk,rhd->khd", grad_scores, q_h, preferred_element_type=f32) * inv_root
    ).reshape(keys_n, cb).astype(bf16)
    grad_v = jnp.einsum("hrk,rhd->khd", probs_low, grad_att_h, preferred_element_type=f32)
    grad_v = grad_v.reshape(keys_n, cb).astype(bf16)
    part_query = mm_tn(hidden_seq, grad_q)
    part_key = mm_tn(context, grad_k)
    part_value = mm_tn(context, grad_v)

    seg_grads = jnp.stack([grad_q, grad_k[2 * seg :], grad_v[2 * seg :]], axis=0)
    own_grads = lax.all_to_all(seg_grads, "tier", 1, 2, tiled=True)
    grad_hidden = grad_resid + mm_nt(own_grads[0], query_weight)
    grad_hidden = grad_hidden + mm_nt(own_grads[1], key_weight)
    grad_hidden = grad_hidden + mm_nt(own_grads[2], value_weight)
    grad_input = grad_hidden * mask_own

    parts = (part_query, part_key, part_value, part_attn_out, part_ffn_in, part_ffn_out, part_comp)
    flat = jnp.concatenate([p.reshape(seqs, -1, width) for p in parts], axis=1)
    flat = flat.reshape(-1, width)
    reduced = lax.psum_scatter(flat, "seq", scatter_dimension=0, tiled=True).reshape(-1)
    outs = []
    start = 0
    for p in parts:
        size = p.size // seqs
        outs.append(reduced[start : start + size].reshape(p.shape[0] // seqs, p.shape[1]))
        start += size

    slope_full = lax.dynamic_update_slice_in_dim(jnp.zeros((heads,), f32), part_slope, tier_pos * hpt, 0)
    gain_total, slope_total = lax.psum((part_gain, slope_full), ("seq", "tier"))
    return (
        output[None],
        grad_input[None],
        hidden_own[None],
        new_compressed[None],
        outs[0],
        outs[1],
        outs[2],
        outs[3],
        outs[4],
        outs[5],
        outs[6],
        gain_total,
        slope_total,
    )


def solution(mesh):
    placed = (
        P("seq", "tier", None),
        P("seq", "tier", None),
        P("seq", "tier", None),
        P("seq"),
        P("seq"),
        P(),
        P(),
        P(),
        P(),
        P(),
        P(),
        P(),
        P(),
        P(),
        P("seq", "tier", None),
    )
    return jax.shard_map(
        per_device,
        mesh=mesh,
        in_specs=placed,
        out_specs=(
            P("seq", "tier", None),
            P("seq", "tier", None),
            P("seq", "tier", None),
            P("seq", "tier", None),
            P("seq", "tier"),
            P("seq", "tier"),
            P("seq", "tier"),
            P("seq", "tier"),
            P("seq", "tier"),
            P("seq", "tier"),
            P("seq", "tier"),
            P(),
            P(),
        ),
        check_vma=False,
    )
```

time: 1540 us -> 495 us (0.32)
  waiting for transfers between devices: 922 us -> 209 us
  blocking collectives: 339 us -> 47.4 us
  other arithmetic: 55.7 us -> 24.3 us
  local copies, waits for them, and re-layouts: 98.8 us -> 69.1 us
    reduce_scatter x14 -> x2, waiting for transfers between devices: 877 us -> 180 us  [the longest x1 180 us: per_device(): lax.psum_scatter(flat, 'seq', scatter_dimension=0, tiled=True).reshape(-1)]
    unnamed x1 -> x0, blocking collectives: 282 us -> none
    unnamed x5 -> x1, other arithmetic: 47.1 us -> 3.13 us
    unnamed x98 -> x93, local copies, waits for them, and re-layouts: 52.8 us -> 22 us
    reshape x0 -> x15, local copies, waits for them, and re-layouts: none -> 23.6 us  [the longest x6 14.1 us: per_device(): flat = jnp.concatenate([p.reshape(seqs, -1, width) for p in parts], axis=1)]
    all_gather x2 -> x3, waiting for transfers between devices: 43.4 us -> 23.7 us  [the longest x1 23.7 us: per_device(): raw_seq = lax.all_gather(raw_local, 'tier', axis=1, tiled=True)]
    dot_general x30 -> x32, matrix products: 99.6 us -> 106 us  [the longest x8 32.5 us: mm(): return jnp.dot(left, right, preferred_element_type=f32)]
  transfers between devices with their start and end apart: 17 -> 8, of which waited for: 13 -> 3; matrix products, arithmetic and copies ran while one was open for 15% -> 30% of each run, Pallas kernels for 0% -> 0%
where the time goes in v1:
time: 495 us; the launch traced here: 487 us
  waiting for transfers between devices  209 us (42%)
  matrix products  110 us (22%)
  local copies, waits for them, and re-layouts  69.1 us (14%)
  blocking collectives  47.4 us (10%)
  other arithmetic  24.3 us (5%)
  between operations  16.3 us (3%)
  starting transfers between devices  10.6 us (2%)
    reduce_scatter x1, waiting for transfers between devices, per_device(): lax.psum_scatter(flat, 'seq', scatter_dimension=0, tiled=True).reshape(-1)  180 us
    psum x1, blocking collectives, per_device(): gain_total, slope_total = lax.psum((part_gain, slope_full), ('seq', 'tier'))  47.4 us
    dot_general x8, matrix products, mm(): return jnp.dot(left, right, preferred_element_type=f32)  32.5 us
    dot_general x6, matrix products, mm_nt(): lax.dot_general(left, right, (((1,), (1,)), ((), ())), preferred_element_...  24.3 us
    all_gather x1, waiting for transfers between devices, per_device(): raw_seq = lax.all_gather(raw_local, 'tier', axis=1, tiled=True)  23.7 us
    unnamed x93, local copies, waits for them, and re-layouts  22 us
    dot_general x7, matrix products, mm_tn(): lax.dot_general(left, right, (((0,), (0,)), ((), ())), preferred_element_...  21.3 us
    reshape x6, local copies, waits for them, and re-layouts, per_device(): flat = jnp.concatenate([p.reshape(seqs, -1, width) for p in parts], axis=1)  14.1 us
  transfers between devices with their start and end apart: 8, of which 3 were waited for; matrix products, arithmetic and copies ran while one was open for 30% of the time, Pallas kernels for 0%

profile of v1, /device:TPU:0, one launch (start us, length us, event | category | flops | bytes accessed | tf_op | source)
XLA Modules:
  0.0 486.8 jit_solution(13463608105993968197)
XLA Ops:
  12.6 3.1 fusion.52
  19.5 23.7 %all-gather.5.cloned.1.call-done = bf16[3,512,1024]{2,1,0:T(8,128)(2,1)} async-done(((bf16[3,128,1024]{2,1,0:T(8,128)(2,1)}), bf16[3,512,1024]{2,1,0:T(8,128)(2,1)}) %all-gather.5.cloned.1.call-update) | async-done | bytes 3145744 | tf_op jit(solution)/shard_map/all_gather | solution.py:83
  43.2 3.7 convolution_convert_fusion
  47.1 2.8 convolution_convert_fusion.5
  57.4 3.4 all-to-all-start
  63.2 2.6 reshape.323
  65.8 4.5 convolution_convert_fusion.2
  82.1 3.1 fusion.54
  92.6 2.6 fusion.93
  97.7 6.0 %fusion.167 = f32[128,4096]{1,0:T(8,128)} fusion(bf16[1024,4096]{1,0:T(8,128)(2,1)} %param.24, f32[128,1024]{1,0:T(8,128)S(1)} %get-tuple-element.44, f32[1024]{0:T(1024)S(1)} %copy-done.38, f32[128]{0:T(128)S(1)} %fusion.135, f32[128]{0:T(128)S(1)} %broadcast_multiply_fusion), kind=kOutput, calls=%fused_computation.219 | convolution fusion | flops 1074266112 | bytes 11015168 | tf_op jit(solution)/shard_map/dot_general | solution.py:31
  103.7 13.9 %multiply_reduce_fusion.4 = (f32[1024]{0:T(1024)S(1)}, f32[128]{0:T(128)S(1)}, f32[128,1024]{1,0:T(8,128)}) fusion(f32[128,1024]{1,0:T(8,128)S(1)} %get-tuple-element.44, f32[128]{0:T(128)S(1)} %fusion.135, f32[128]{0:T(128)S(1)} %broadcast_multiply_fusion, f32[1024]{0:T(1024)S(1)} %copy-done.38, bf16[1024,4096]{1,0:T(8,128)(2,1)} %param.24, ...), kind=kOutput, calls=%fused_computation.135 | convolution fusion | flops 2159279104 | bytes 20195328 | tf_op jit(solution)/shard_map/dot_general | solution.py:39
  123.5 3.5 all-to-all-start.1
  127.1 2.5 fusion.32
  130.7 5.1 %all-to-all-done.1 = bf16[2,128,1024]{1,0,2:T(2,128)(2,1)S(1)} async-done(((bf16[2,128,1024]{1,0,2:T(2,128)(2,1)}), bf16[2,128,1024]{1,0,2:T(2,128)(2,1)S(1)}, u32[]{:S(2)}, u32[]{:S(2)}) %all-to-all-start.1) | async-done | bytes 524320 | tf_op jit(solution)/shard_map/all_to_all | solution.py:171
  137.0 4.9 %multiply_reduce_fusion.1 = (f32[2,512]{1,0:T(2,128)S(1)}, f32[2,512,1536]{2,1,0:T(8,128)S(1)}) fusion(f32[2,512,1536]{2,1,0:T(8,128)} %copy-done.2, f32[2,512]{1,0:T(2,128)S(1)} %log_add_fusion, bf16[512,2,128]{0,2,1:T(8,128)(2,1)S(1)} %reshape.348, bf16[1536,2,128]{0,2,1:T(8,128)(2,1)S(1)} %bitcast.169), kind=kOutput, calls=%fused_computation.13 | convolution fusion | flops 407370752 | bytes 13639680 | tf_op jit(solution)/shard_map/rhd,khd->hrk/dot_general | solution.py:193
  141.9 4.7 multiply_reduce_fusion
  152.6 2.6 fusion.17
  157.8 4.2 convolution_convert_fusion.1
  171.1 3.2 fusion.117
  174.3 4.8 reshape.333
  183.8 7.3 %fusion.63 = f32[512,4096]{1,0:T(8,128)S(1)} fusion(bf16[1024,4096]{1,0:T(8,128)(2,1)} %param.24, bf16[2,512,1024]{2,1,0:T(8,128)(2,1)} %all-gather.7.cloned.1.call-done), kind=kOutput, calls=%fused_computation.98 | convolution fusion | flops 4294967296 | bytes 17825792 | tf_op jit(solution)/shard_map/dot_general | solution.py:31
  191.1 3.3 copy-done.41
  194.4 4.7 fusion.11
  199.1 5.2 %reshape.328 = f32[8,128,1024]{2,1,0:T(8,128)} reshape(f32[4096,256]{1,0:T(8,128)} %fusion.11) | data formatting | bytes 8388608 | tf_op jit(solution)/shard_map/reshape | solution.py:216
  205.4 7.7 %convolution_dynamic-update-slice_fusion = f32[8,480,1024]{2,1,0:T(8,128)} fusion(f32[8,480,1024]{2,1,0:T(8,128)} %constant_dynamic-update-slice_fusion.2, bf16[8,128,512]{2,1,0:T(8,128)(2,1)} %bitcast.187, f32[512,4096]{1,0:T(8,128)} %copy-done.41, s32[]{:T(128)S(6)} %select_n.37, bf16[512,1024]{1,0:T(8,128)(2,1)S(1)} %copy-done.24, ...), kind=kOutput, calls=%fused_computation.30 | convolution fusion | flops 2157969408 | bytes 10486784 | tf_op jit(solution)/shard_map/dot_general | solution.py:35
  213.1 4.9 %constant_dynamic-update-slice_fusion.1 = f32[8,480,1024]{2,1,0:T(8,128)} fusion(f32[8,480,1024]{2,1,0:T(8,128)} %convolution_dynamic-update-slice_fusion, f32[8,128,1024]{2,1,0:T(8,128)} %reshape.328), kind=kLoop, calls=%fused_computation.164 | loop fusion | bytes 8388608
  224.6 2.8 pad_maximum_fusion.1
  227.4 3.5 all-to-all-start.2
  230.9 6.3 %fusion.56 = bf16[1,128,1024]{2,1,0:T(8,128)(2,1)} fusion(f32[128,1024]{1,0:T(8,128)S(1)} %get-tuple-element.44, bf16[4096,1024]{1,0:T(8,128)(2,1)} %param.25, f32[128,4096]{1,0:T(8,128)} %fusion.167, f32[128]{0:T(128)S(1)} %compare_convert_fusion), kind=kOutput, calls=%fused_computation.83 | convolution fusion | flops 1078853632 | bytes 11272704 | tf_op jit(solution)/shard_map/dot_general | solution.py:31
  237.3 47.4 %all-reduce.1 = (f32[1024]{0:T(1024)}, f32[8]{0:T(128)}) all-reduce(f32[1024]{0:T(1024)S(1)} %get-tuple-element.13, f32[8]{0:T(128)S(1)} %negate_dynamic-update-slice_fusion), channel_id=1, replica_groups=mesh['seq'=8,'tier'=4] {'seq','tier'}, use_global_device_ids=true, to_apply=%region_15.16 | all-reduce | flops 1032 | bytes 8256 | tf_op jit(solution)/shard_map/psum | solution.py:227
  285.4 2.9 convolution_add_fusion.2
  292.4 179.6 %reduce-scatter.5.cloned.1.call-done = f32[480,1024]{1,0:T(8,128)} async-done(((f32[3840,1024]{1,0:T(8,128)}), f32[480,1024]{1,0:T(8,128)}) %reduce-scatter.5.cloned.1.call-update) | async-done | bytes 1966096 | tf_op jit(solution)/shard_map/reduce_scatter | solution.py:218
  (194 shorter events, 90.0 us)
Async XLA Ops:
  7.2 88.7 %copy-start = (bf16[1024,1024]{1,0:T(8,128)(2,1)S(1)}, bf16[1024,1024]{1,0:T(8,128)(2,1)}, u32[]{:S(2)}) copy-start(bf16[1024,1024]{1,0:T(8,128)(2,1)} %param.23) | copy-start | bytes 6291460
  7.2 36.0 %all-gather.5.cloned.1.call-start = ((), (), s32[]{:S(2)}) async-start(), calls=%async_computation.5 | async-start | bytes 3932160 | tf_op jit(solution)/shard_map/all_gather | solution.py:83
  11.8 115.3 %all-gather.9.cloned.1.call-start = ((), (), s32[]{:S(2)}) async-start(), calls=%async_computation.9 | async-start | bytes 1310720 | tf_op jit(solution)/shard_map/all_gather | solution.py:84
  19.5 23.7 %copy-start.33 = (bf16[1024,256]{1,0:T(8,128)(2,1)}, bf16[1024,256]{1,0:T(8,128)(2,1)S(1)}, u32[]{:S(2)}) copy-start(bf16[1024,256]{1,0:T(8,128)(2,1)S(1)} %get-tuple-element.53) | copy-start | bytes 1572868
  19.5 27.4 %copy-start.31 = (bf16[1024,256]{1,0:T(8,128)(2,1)}, bf16[1024,256]{1,0:T(8,128)(2,1)S(1)}, u32[]{:S(2)}) copy-start(bf16[1024,256]{1,0:T(8,128)(2,1)S(1)} %get-tuple-element.52) | copy-start | bytes 1572868
  47.1 6.6 %copy-start.7 = (bf16[1536,256]{0,1:T(8,128)(2,1)}, bf16[1536,256]{0,1:T(8,128)(2,1)S(1)}, u32[]{:S(2)}) copy-start(bf16[1536,256]{0,1:T(8,128)(2,1)S(1)} %get-tuple-element.30) | copy-start | bytes 2359300
  57.4 37.8 %all-to-all-start = ((bf16[4,128,256]{1,2,0:T(8,128)(2,1)}), bf16[4,128,256]{1,2,0:T(8,128)(2,1)S(1)}, u32[]{:S(2)}, u32[]{:S(2)}) async-start(bf16[4,128,256]{1,2,0:T(8,128)(2,1)} %copy.122), calls=%async_computation | async-start | bytes 524288 | tf_op jit(solution)/shard_map/all_to_all | solution.py:117
  60.8 110.3 %reduce-scatter.3.cloned.1.call-start = ((), (), s32[]{:S(2)}) async-start(), calls=%async_computation.7 | async-start | bytes 901120 | tf_op jit(solution)/shard_map/reduce_scatter | solution.py:145
  65.8 4.5 copy-start.32
  65.8 4.5 copy-start.34
  65.8 7.5 %copy-start.29 = (bf16[512,256]{0,1:T(8,128)(2,1)S(1)}, bf16[512,256]{0,1:T(8,128)(2,1)}, u32[]{:S(2)}) copy-start(bf16[512,256]{0,1:T(8,128)(2,1)} %copy-done.28) | copy-start | bytes 786436
  92.5 5.1 %copy-start.38 = (f32[1024]{0:T(1024)S(1)}, f32[1024]{0:T(1024)}, u32[]{:S(2)}) copy-start(f32[1024]{0:T(1024)} %param.26) | copy-start | bytes 12292
  122.4 7.3 %copy-start.21 = (bf16[4,128,256]{1,2,0:T(8,128)(2,1)S(1)}, bf16[4,128,256]{1,2,0:T(8,128)(2,1)}, u32[]{:S(2)}) copy-start(bf16[4,128,256]{1,2,0:T(8,128)(2,1)} %copy-done.20) | copy-start | bytes 786436
  122.4 7.4 %copy-start.27 = (bf16[1,128,1024]{2,1,0:T(8,128)(2,1)S(1)}, bf16[1,128,1024]{2,1,0:T(8,128)(2,1)}, u32[]{:S(2)}) copy-start(bf16[1,128,1024]{2,1,0:T(8,128)(2,1)} %get-tuple-element.34) | copy-start | bytes 786436
  123.5 12.3 %all-to-all-start.1 = ((bf16[2,128,1024]{1,0,2:T(2,128)(2,1)}), bf16[2,128,1024]{1,0,2:T(2,128)(2,1)S(1)}, u32[]{:S(2)}, u32[]{:S(2)}) async-start(bf16[2,128,1024]{1,0,2:T(2,128)(2,1)} %copy.123), calls=%async_computation.1 | async-start | bytes 1048576 | tf_op jit(solution)/shard_map/all_to_all | solution.py:171
  127.0 52.2 %all-gather.7.cloned.1.call-start = ((), (), s32[]{:S(2)}) async-start(), calls=%async_computation.6 | async-start | bytes 2621440 | tf_op jit(solution)/shard_map/all_gather | solution.py:175
  129.6 7.4 %copy-start.8 = (bf16[1536,256]{0,1:T(8,128)(2,1)S(1)}, bf16[1536,256]{0,1:T(8,128)(2,1)}, u32[]{:S(2)}) copy-start(bf16[1536,256]{0,1:T(8,128)(2,1)} %copy-done.7) | copy-start | bytes 2359300
  130.6 341.4 %reduce-scatter.5.cloned.1.call-start = ((), (), s32[]{:S(2)}) async-start(), calls=%async_computation.8 | async-start | bytes 17694720 | tf_op jit(solution)/shard_map/reduce_scatter | solution.py:218
  137.0 4.9 %copy-start.4 = (f32[1536,512]{0,1:T(8,128)S(1)}, f32[1536,512]{0,1:T(8,128)}, u32[]{:S(2)}) copy-start(f32[1536,512]{0,1:T(8,128)} %get-tuple-element.39) | copy-start | bytes 9437188
  149.4 5.8 %copy-start.18 = (bf16[2,128,512]{2,1,0:T(8,128)(2,1)}, bf16[2,128,512]{2,1,0:T(8,128)(2,1)S(1)}, u32[]{:S(2)}) copy-start(bf16[2,128,512]{2,1,0:T(8,128)(2,1)S(1)} %fusion.50) | copy-start | bytes 786436
  165.2 4.8 copy-start.12
  165.2 5.9 %copy-start.11 = (bf16[171,3072]{1,0:T(8,128)(2,1)S(1)}, bf16[171,3072]{1,0:T(8,128)(2,1)}, u32[]{:S(2)}) copy-start(bf16[171,3072]{1,0:T(8,128)(2,1)} %reshape.323) | copy-start | bytes 3151876
  174.3 4.9 copy-start.37
  183.8 10.6 %copy-start.24 = (bf16[512,1024]{1,0:T(8,128)(2,1)S(1)}, bf16[512,1024]{1,0:T(8,128)(2,1)}, u32[]{:S(2)}) copy-start(bf16[512,1024]{1,0:T(8,128)(2,1)} %fusion.32) | copy-start | bytes 3145732
  213.1 4.9 %copy-start.5 = (f32[8,96,1024]{2,1,0:T(8,128)S(1)}, f32[8,96,1024]{2,1,0:T(8,128)}, u32[]{:S(2)}) copy-start(f32[8,96,1024]{2,1,0:T(8,128)} %reshape.333) | copy-start | bytes 9437188
  219.9 4.3 copy-start.19
  227.4 57.3 %all-to-all-start.2 = ((bf16[3,512,256]{2,0,1:T(4,128)(2,1)}), bf16[3,512,256]{2,0,1:T(4,128)(2,1)S(1)}, u32[]{:S(2)}, u32[]{:S(2)}) async-start(bf16[3,512,256]{2,0,1:T(4,128)(2,1)} %pad_maximum_fusion.1), calls=%async_computation.2 | async-start | bytes 2097152 | tf_op jit(solution)/shard_map/all_to_all | solution.py:209
  237.2 48.2 %copy-start.10 = (f32[128,1024]{1,0:T(8,128)S(1)}, f32[128,1024]{1,0:T(8,128)}, u32[]{:S(2)}) copy-start(f32[128,1024]{1,0:T(8,128)} %copy-done.9) | copy-start | bytes 1572868
  237.2 48.2 %copy-start.22 = (bf16[1,128,1024]{2,1,0:T(8,128)(2,1)S(1)}, bf16[1,128,1024]{2,1,0:T(8,128)(2,1)}, u32[]{:S(2)}) copy-start(bf16[1,128,1024]{2,1,0:T(8,128)(2,1)} %param.29) | copy-start | bytes 786436
  285.4 5.3 %copy-start.13 = (bf16[1024,1024]{1,0:T(8,128)(2,1)S(1)}, bf16[1024,1024]{1,0:T(8,128)(2,1)}, u32[]{:S(2)}) copy-start(bf16[1024,1024]{1,0:T(8,128)(2,1)} %param.22) | copy-start | bytes 6291460
  472.1 7.1 %slice-start = ((f32[480,1024]{1,0:T(8,128)}), f32[96,1024]{1,0:T(8,128)S(1)}, s32[]{:S(2)}) async-start(f32[480,1024]{1,0:T(8,128)} %reduce-scatter.5.cloned.1.call-done), calls=%async_computation.10 | async-start | bytes 786432 | tf_op jit(solution)/shard_map/slice | solution.py:223
  472.1 7.9 %copy-start.1 = (bf16[1024,1024]{1,0:T(8,128)(2,1)S(1)}, bf16[1024,1024]{1,0:T(8,128)(2,1)}, u32[]{:S(2)}) copy-start(bf16[1024,1024]{1,0:T(8,128)(2,1)} %param.23) | copy-start | bytes 6291460
  (19 other events, 46.1 us)
Sparse Core Ops, SparseCore 0:
  12.0 31.2 all-gather.4
  44.8 16.7 all-gather.8
  95.3 24.2 reduce-scatter.2
  130.8 23.9 all-gather.6
  220.0 251.9 reduce-scatter.4
